TPU v7x, 256 devices: a whole 4x4x8 slice. The times are simulated.
256 devices in a mesh: tm: 32 (over y, x, core), space: 8 (over z).
Axes of the slice: x: 4, y: 4, z: 8, core: 2. Of those that a mesh axis runs over, the one named last changes fastest.
Arguments:
- latent_tokens: bfloat16 [64, 1792, 2240], P('tm', 'space'), may hold values from -6 to 6
- norm_gain: float32 [2240], replicated, may hold values from 0.5 to 1.5
- w_query: bfloat16 [2240, 1120], P('tm', 'space'), may hold values from -0.125 to 0.125
- w_key: bfloat16 [2240, 1120], P('tm', 'space'), may hold values from -0.125 to 0.125
- w_value: bfloat16 [2240, 1120], P('tm', 'space'), may hold values from -0.125 to 0.125
- out_gain: float32 [1120], replicated, may hold values from 0.5 to 1.5
- block_ids: int32 [64], P('tm'), may hold values from 0 to 15, never falling along the last dimension, each value on 1 to 8 neighbouring positions
Outputs:
- attended: bfloat16 [64, 1792, 1120], P('tm', 'space')
Inputs may be any that keep to these rules, and one draw needn't show every extreme that they name: `block_ids`: block numbers never fall from one frame to the next; each of the 16 blocks holds 1 to 8 frames and one holds exactly 8.
All inputs are finite; a program needn't handle non-finite values.
Results may differ from a plain program's by a relative error of at most 0.0065.
Values may be sent and summed in bfloat16 or wider, within the bound.
A program may use at most 192 MiB of HBM per device.

v0:
```python
import jax
import jax.numpy as jnp
from jax import lax
from jax.sharding import PartitionSpec as P

HEAD = 112
HEADS = 10


def prefix(value, axis, join, neutral):
    count, mine = (lax.axis_size(axis), lax.axis_index(axis))
    pieces = lax.all_gather(value, axis)
    so_far = jnp.full_like(value, 0) + jnp.asarray(neutral, value.dtype)

    def step(position, so_far):
        longer = join(so_far, pieces[position])
        return jnp.where(position < mine, longer, so_far)

    return lax.fori_loop(0, count - 1, step, so_far)


def carried_in(x, axis, join, neutral):
    count = lax.axis_size(axis)
    place = lax.axis_index(axis)
    ahead = count - 1 - place
    gathered = jax.tree.map(
        lambda a, kind: lax.all_gather(a.astype(kind), axis),
        x,
        jax.tree.map(lambda a: jnp.bfloat16 if a.dtype == jnp.float32 else a.dtype, x),
    )
    state = jax.tree.map(lambda a, e: jnp.zeros_like(a) + jnp.asarray(e, a.dtype), x, neutral)

    def one(step, state):
        source = count - 1 - step
        return join(
            state,
            jax.tree.map(
                lambda a, own: lax.dynamic_index_in_dim(a, source, 0, False).astype(own.dtype),
                gathered,
                x,
            ),
        )

    return lax.fori_loop(0, ahead, one, state)


def add_states(earlier, later):
    return earlier + later


def join_later(earlier, later):
    high_vacant, high_leading, high_uniform, high_running = earlier
    low_vacant, low_leading, low_uniform, low_running = later
    matching = (high_leading == low_leading).astype(jnp.float32)
    joined = low_uniform * matching * (1.0 - high_vacant)
    low_absent = low_vacant > 0.5
    leading = jnp.where(low_absent, high_leading, low_leading)
    vacant = low_vacant * high_vacant
    uniform = jnp.where(
        low_absent,
        high_uniform,
        low_uniform * (high_vacant + (1.0 - high_vacant) * high_uniform * matching),
    )
    running = jnp.where(low_absent, high_running, low_running + joined * high_running)
    return (vacant, leading, uniform, running)


def on_device(latent_tokens, norm_gain, w_query, w_key, w_value, out_gain, block_ids):
    frame_count, token_count, width = latent_tokens.shape
    row_count = frame_count * token_count
    values = latent_tokens.reshape(row_count, width).astype(jnp.float32)
    meansq = jnp.mean(values * values, axis=-1, keepdims=True)
    normed = (values * lax.rsqrt(meansq + 1e-06) * norm_gain).astype(jnp.bfloat16)
    stacked = jnp.stack((w_query, w_key, w_value))
    columns_full = lax.all_gather(stacked, "space", axis=2, tiled=True)
    projected = jnp.einsum(
        "rn,cnh->crh",
        normed,
        lax.all_gather(columns_full, "tm", axis=1, tiled=True),
        preferred_element_type=jnp.float32,
    )
    channels = projected.shape[2]
    query = jax.nn.relu(projected[0]).reshape(frame_count, token_count, HEADS, HEAD)
    key = (
        jax.nn.relu(projected[1])
        .astype(jnp.bfloat16)
        .reshape(frame_count, token_count, HEADS, HEAD)
    )
    value = projected[2].astype(jnp.bfloat16).reshape(frame_count, token_count, HEADS, HEAD)
    local_states = jnp.einsum("fthk,fthv->fhkv", key, value, preferred_element_type=jnp.float32)
    per_frame_state = lax.psum(local_states, "space")
    device_sum = jnp.sum(per_frame_state, axis=0)
    zero_state = jnp.zeros_like(device_sum)
    before = prefix(device_sum, "tm", add_states, zero_state)
    leading_id = block_ids[0]
    closing_id = block_ids[frame_count - 1]
    within_leading = (block_ids == leading_id).astype(jnp.float32)
    leading_sum = jnp.einsum(
        "o,owpe->wpe", within_leading, per_frame_state, precision=lax.Precision.HIGHEST
    )
    uniform_flag = jnp.min(within_leading)
    leading_float = leading_id.astype(jnp.float32)
    closing_float = closing_id.astype(jnp.float32)
    summary = (jnp.float32(0.0), leading_float, uniform_flag, leading_sum)
    identity = (jnp.float32(1.0), jnp.float32(0.0), jnp.float32(1.0), zero_state)
    vacant, leading, uniform, running = carried_in(summary, "tm", join_later, identity)
    reaches = (1.0 - vacant) * (leading == closing_float).astype(jnp.float32)
    trailing = reaches * running
    earlier_mask = (block_ids[None, :] <= block_ids[:, None]).astype(jnp.float32)
    in_closing = (block_ids == closing_id).astype(jnp.float32)
    carried = before[None] + jnp.einsum(
        "ij,jhkv->ihkv", earlier_mask, per_frame_state, precision=lax.Precision.HIGHEST
    )
    carried = carried + in_closing[:, None, None, None] * trailing[None]
    numerator = jnp.einsum("fthk,fhkv->fthv", query, carried, precision=lax.Precision.HIGHEST)
    head_meansq = jnp.mean(numerator * numerator, axis=-1, keepdims=True)
    result = numerator * lax.rsqrt(head_meansq + 1e-06) * out_gain.reshape(HEADS, HEAD)
    return result.reshape(frame_count, token_count, channels).astype(jnp.bfloat16)


def solution(mesh):
    placed = (
        P("tm", "space", None),
        P(),
        P("tm", "space"),
        P("tm", "space"),
        P("tm", "space"),
        P(),
        P("tm"),
    )
    return jax.shard_map(
        on_device, mesh=mesh, in_specs=placed, out_specs=P("tm", "space", None), check_vma=False
    )
```

profile of v0, /device:TPU:32, one launch (start us, length us, event | category | flops | bytes accessed | tf_op | source)
XLA Modules:
  0.0 544.3 jit_solution(14924308415363143273)
XLA Ops:
  7.7 29.9 %all_gather.33 = bf16[3,70,1120]{1,0,2:T(4,128)(2,1)S(1)} all-gather(bf16[3,70,140]{1,0,2:T(4,128)(2,1)S(1)} %copy.37), channel_id=1, replica_groups=mesh['tm'=32,'space'=8] {'space'}, dimensions={2}, use_global_device_ids=true | all-gather | bytes 529200 | tf_op jit(solution)/shard_map/all_gather | solution.py:75
  37.6 2.2 copy.38
  40.5 1.9 fusion.7
  42.4 84.1 %all-gather.6.cloned.1.call-done = bf16[3,2240,1120]{2,0,1:T(4,128)(2,1)} async-done(((bf16[3,70,1120]{2,0,1:T(4,128)(2,1)}), bf16[3,2240,1120]{2,0,1:T(4,128)(2,1)}) %all-gather.6.cloned.1.call-update) | async-done | bytes 15052816 | tf_op jit(solution)/shard_map/all_gather | solution.py:79
  126.5 14.1 %fusion.3 = f32[3,448,1120]{2,1,0:T(8,128)S(1)} fusion(bf16[3,2240,1120]{2,0,1:T(4,128)(2,1)} %all-gather.6.cloned.1.call-done, bf16[448,2240]{1,0:T(8,128)(2,1)} %fusion.7), kind=kOutput, calls=%fused_computation.5 | convolution fusion | flops 6743654400 | bytes 23080960 | tf_op jit(solution)/shard_map/rn,cnh->crh/dot_general | solution.py:76
  140.7 1.4 fusion.13
  142.1 1.5 copy-done.2
  143.6 3.4 reshape.84
  147.0 3.1 reshape.83
  150.1 3.1 fusion.16
  153.9 75.4 %all-reduce.6.cloned.1.call-done = f32[2,10,112,112]{3,2,1,0:T(8,128)} async-done(((f32[2,10,112,112]{3,2,1,0:T(8,128)}), f32[2,10,112,112]{3,2,1,0:T(8,128)}) %all-reduce.6.cloned.1.call-update) | async-done | bytes 1003536 | tf_op jit(solution)/shard_map/psum | solution.py:91
  229.3 4.7 fusion.20
  238.5 1.2 fusion.27
  239.7 1.3 dynamic-update-slice.2
  241.0 63.4 %all-reduce.3 = (bf16[32]{0:T(256)(128)(2,1)S(1)}, bf16[32]{0:T(256)(128)(2,1)S(1)}, bf16[32]{0:T(256)(128)(2,1)S(1)}) all-reduce(bf16[32]{0:T(256)(128)(2,1)S(1)} %dynamic-update-slice, bf16[32]{0:T(256)(128)(2,1)S(1)} %dynamic-update-slice.1, bf16[32]{0:T(256)(128)(2,1)S(1)} %dynamic-update-slice.2), channel_id=1, replica_groups=mesh['tm'=32,'space'=8] {'tm'}, use_global_device_ids=true, to_apply=%add | all-reduce | flops 96 | bytes 384
  305.6 1.7 slice_maximum_fusion
  307.4 3.3 reshape.85
  310.7 177.9 %while.32 = (s32[]{:T(128)}, f32[]{:T(128)}, f32[]{:T(128)}, f32[10,112,112]{2,1,0:T(8,128)S(1)}, s32[]{:T(128)}, /*index=5*/bf16[32]{0:T(256)(128)(2,1)S(1)}, b...) while((s32[]{:T(128)}, f32[]{:T(128)}, f32[]{:T(128)}, ...), condition=%wide.region_7.8_spmd, body=%wide.region_6.7_spmd.sunk | while | flops 501773 | bytes 1254722 | solution.py:44
  315.2 1.3 fusion.33
  320.9 1.3 fusion.33
  326.6 1.3 fusion.33
  332.4 1.3 fusion.33
  338.1 1.3 fusion.33
  343.9 1.3 fusion.33
  349.6 1.3 fusion.33
  355.3 1.3 fusion.33
  361.1 1.3 fusion.33
  366.8 1.3 fusion.33
  372.6 1.3 fusion.33
  378.3 1.3 fusion.33
  384.0 1.3 fusion.33
  389.8 1.3 fusion.33
  395.5 1.3 fusion.33
  401.2 1.3 fusion.33
  407.0 1.3 fusion.33
  412.7 1.3 fusion.33
  418.4 1.3 fusion.33
  424.2 1.3 fusion.33
  429.9 1.3 fusion.33
  435.6 1.3 fusion.33
  441.4 1.3 fusion.33
  447.1 1.3 fusion.33
  452.9 1.3 fusion.33
  458.6 1.3 fusion.33
  464.3 1.3 fusion.33
  470.1 1.3 fusion.33
  475.8 1.3 fusion.33
  481.5 1.3 fusion.33
  487.3 1.3 fusion.33
  488.6 38.9 %while.33 = (s32[]{:T(128)}, f32[10,112,112]{2,1,0:T(8,128)S(1)}, s32[]{:T(128)}, f32[32,10,112,112]{3,2,1,0:T(8,128)}, s32[]{:T(128)}, /*index=5*/s32[]{:T(128)}) while((s32[]{:T(128)}, f32[10,112,112]{2,1,0:T(8,128)S(1)}, s32[]{:T(128)}, f32[32,10,112,112]{3,2,1,0:T(8,128)}, s32[]{:T(128)}, /*index=5*/s32[]{:T(128)}) %tuple.73), condition=%wide.region_4.5_spmd.clone, body=%wide.region_3.4_spmd.clone.sunk | while | flops 376324 | bytes 1505381 | solution.py:19
  488.6 1.3 add_select_fusion.2
  490.0 1.2 add_select_fusion.2
  491.2 1.2 add_select_fusion.2
  492.5 1.2 add_select_fusion.2
  493.7 1.2 add_select_fusion.2
  495.0 1.2 add_select_fusion.2
  496.3 1.2 add_select_fusion.2
  497.5 1.2 add_select_fusion.2
  498.8 1.2 add_select_fusion.2
  500.0 1.2 add_select_fusion.2
  523.8 1.2 add_select_fusion.2
  527.6 3.3 fusion.15
  530.9 5.1 fusion.8
  536.4 1.4 copy.48
  (161 shorter events, 83.9 us)
Async XLA Ops:
  6.5 120.0 %all-gather.6.cloned.1.call-start = ((), (), s32[]{:S(2)}) async-start(), calls=%async_computation | async-start | bytes 21288960 | tf_op jit(solution)/shard_map/all_gather | solution.py:79
  6.5 33.4 %copy-start.1 = (bf16[2,224,2240]{2,1,0:T(8,128)(2,1)S(1)}, bf16[2,224,2240]{2,1,0:T(8,128)(2,1)}, u32[]{:S(2)}) copy-start(bf16[2,224,2240]{2,1,0:T(8,128)(2,1)} %param.11) | copy-start | bytes 6021124
  37.6 2.9 copy-start.5
  39.9 189.4 %all-reduce.6.cloned.1.call-start = ((), (), s32[]{:S(2)}) async-start(), calls=%async_computation.1 | async-start | bytes 2293760 | tf_op jit(solution)/shard_map/psum | solution.py:91
  140.7 2.9 copy-start.2
  150.1 3.2 copy-start.7
  153.3 157.4 %all-gather.10.cloned.1.call-start = ((), (), s32[]{:S(2)}) async-start(), calls=%async_computation.3 | async-start | bytes 9461760 | tf_op jit(solution)/shard_map/all_gather | solution.py:27
  229.3 5.6 %copy-start.3 = (f32[2,10,112,112]{3,2,1,0:T(8,128)S(1)}, f32[2,10,112,112]{3,2,1,0:T(8,128)}, u32[]{:S(2)}) copy-start(f32[2,10,112,112]{3,2,1,0:T(8,128)} %all-reduce.6.cloned.1.call-done) | copy-start | bytes 3010564
  234.0 2.5 copy-start.8
  234.0 71.0 %copy-start.6 = (f32[1120]{0:T(1024)S(1)}, f32[1120]{0:T(1024)}, u32[]{:S(2)}) copy-start(f32[1120]{0:T(1024)} %param.16) | copy-start | bytes 13444
  234.8 253.8 %all-gather.8.cloned.1.call-start = ((), (), s32[]{:S(2)}) async-start(), calls=%async_computation.2 | async-start | bytes 18923520 | tf_op jit(solution)/shard_map/all_gather | solution.py:12
  488.6 38.9 %copy-start.4 = (f32[2,10,112,112]{3,2,1,0:T(8,128)S(1)}, f32[2,10,112,112]{3,2,1,0:T(8,128)}, u32[]{:S(2)}) copy-start(f32[2,10,112,112]{3,2,1,0:T(8,128)} %all-reduce.6.cloned.1.call-done) | copy-start | bytes 3010564
  527.6 3.3 copy-start
Sparse Core Ops, SparseCore 0:
  40.0 86.5 all-gather.5
  153.4 75.8 all-reduce.5
  235.0 58.7 all-gather.9
  296.1 80.6 all-gather.7
where the time goes:
time: 548 us; the launch traced here: 544 us
  waiting for transfers between devices  160 us (29%)
  blocking collectives  93.3 us (17%)
  loops' own time  87.7 us (16%)
  other arithmetic  87.5 us (16%)
  local copies, waits for them, and re-layouts  71.2 us (13%)
  matrix products  30.4 us (6%)
  between operations  14.5 us (3%)
    another operation x1, loops' own time, carried_in(): return lax.fori_loop(0, ahead, one, state)  86.9 us
    all_gather x1, waiting for transfers between devices, on_device(): lax.all_gather(columns_full, 'tm', axis=1, tiled=True)  84.1 us
    psum x1, waiting for transfers between devices, on_device(): per_frame_state = lax.psum(local_states, 'space')  75.4 us
    unnamed x1, blocking collectives  63.4 us
    dynamic_slice x93, local copies, waits for them, and re-layouts, one(): lax.dynamic_index_in_dim(a, source, 0, False).astype(own.dtype)  52 us
    select_n x31, other arithmetic, join_later(): jnp.where(low_absent, high_running, low_running + joined * high_running)  38.9 us
    select_n x31, other arithmetic, step(): return jnp.where(position < mine, longer, so_far)  38.2 us
    all_gather x1, blocking collectives, on_device(): columns_full = lax.all_gather(stacked, 'space', axis=2, tiled=True)  29.9 us
  transfers between devices with their start and end apart: 4, of which 2 were waited for; matrix products, arithmetic and copies ran while one was open for 19% of the time, Pallas kernels for 0%

commit v1 on v0

--- a/solution.py
+++ b/solution.py
@@ -5,6 +5,13 @@
 
 HEAD = 112
 HEADS = 10
+
+
+def unite_the_hubs(point, dim_at):
+    k_all = lax.axis_size("tm")
+    vals = [k_all if q == dim_at else 1 for q in range(point.ndim)]
+    response = jnp.tile(point, vals)
+    return lax.all_to_all(response, "tm", split_axis=dim_at, concat_axis=dim_at, tiled=True)
 
 
 def prefix(value, axis, join, neutral):
@@ -74,10 +81,7 @@
     stacked = jnp.stack((w_query, w_key, w_value))
     columns_full = lax.all_gather(stacked, "space", axis=2, tiled=True)
     projected = jnp.einsum(
-        "rn,cnh->crh",
-        normed,
-        lax.all_gather(columns_full, "tm", axis=1, tiled=True),
-        preferred_element_type=jnp.float32,
+        "rn,cnh->crh", normed, unite_the_hubs(columns_full, 1), preferred_element_type=jnp.float32
     )
     channels = projected.shape[2]
     query = jax.nn.relu(projected[0]).reshape(frame_count, token_count, HEADS, HEAD)

time: 548 us -> 751 us (1.37)
  waiting for transfers between devices: 160 us -> 332 us
  loops' own time: 87.7 us -> 99.1 us
  local copies, waits for them, and re-layouts: 71.2 us -> 81.7 us
  starting transfers between devices: 0.13 us -> 7.87 us
    all_to_all x0 -> x1, waiting for transfers between devices: none -> 261 us  [unite_the_hubs(): lax.all_to_all(response, 'tm', split_axis=dim_at, concat_axis=dim_at, til...]
    all_gather x1 -> x0, waiting for transfers between devices: 84.1 us -> none  [on_device(): lax.all_gather(columns_full, 'tm', axis=1, tiled=True)]
    another operation x1, loops' own time: 86.9 us -> 98.3 us  [carried_in(): return lax.fori_loop(0, ahead, one, state)]
    all_to_all x0 -> x1, starting transfers between devices: none -> 7.56 us  [unite_the_hubs(): lax.all_to_all(response, 'tm', split_axis=dim_at, concat_axis=dim_at, til...]
  transfers between devices with their start and end apart: 4 -> 4, of which waited for: 2 -> 2; matrix products, arithmetic and copies ran while one was open for 19% -> 15% of each run, Pallas kernels for 0% -> 0%
where the time goes in v1:
time: 751 us; the launch traced here: 746 us
  waiting for transfers between devices  332 us (44%)
  loops' own time  99.1 us (13%)
  blocking collectives  93.3 us (12%)
  other arithmetic  87.7 us (12%)
  local copies, waits for them, and re-layouts  81.7 us (11%)
  matrix products  30.3 us (4%)
  between operations  14.7 us (2%)
  starting transfers between devices  7.87 us (1%)
    all_to_all x1, waiting for transfers between devices, unite_the_hubs(): lax.all_to_all(response, 'tm', split_axis=dim_at, concat_axis=dim_at, til...  261 us
    another operation x1, loops' own time, carried_in(): return lax.fori_loop(0, ahead, one, state)  98.3 us
    psum x1, waiting for transfers between devices, on_device(): per_frame_state = lax.psum(local_states, 'space')  70.7 us
    unnamed x1, blocking collectives  63.4 us
    dynamic_slice x93, local copies, waits for them, and re-layouts, one(): lax.dynamic_index_in_dim(a, source, 0, False).astype(own.dtype)  55.8 us
    select_n x31, other arithmetic, join_later(): jnp.where(low_absent, high_running, low_running + joined * high_running)  39.1 us
    select_n x31, other arithmetic, step(): return jnp.where(position < mine, longer, so_far)  38.2 us
    all_gather x1, blocking collectives, on_device(): columns_full = lax.all_gather(stacked, 'space', axis=2, tiled=True)  29.9 us
  transfers between devices with their start and end apart: 4, of which 2 were waited for; matrix products, arithmetic and copies ran while one was open for 15% of the time, Pallas kernels for 0%

profile of v1, /device:TPU:32, one launch (start us, length us, event | category | flops | bytes accessed | tf_op | source)
XLA Modules:
  0.0 746.4 jit_solution(4015341823566589168)
XLA Ops:
  7.6 29.9 %all_gather.30 = bf16[3,70,1120]{1,0,2:T(4,128)(2,1)S(1)} all-gather(bf16[3,70,140]{1,0,2:T(4,128)(2,1)S(1)} %copy.38), channel_id=1, replica_groups=mesh['tm'=32,'space'=8] {'space'}, dimensions={2}, use_global_device_ids=true | all-gather | bytes 529200 | tf_op jit(solution)/shard_map/all_gather | solution.py:82
  37.4 1.5 copy.61
  39.0 7.3 tile.4.clone
  46.2 7.6 %all-to-all-start = ((bf16[3,2240,1120]{2,0,1:T(4,128)(2,1)}), bf16[3,2240,1120]{2,0,1:T(4,128)(2,1)}, u32[]{:S(2)}, u32[]{:S(2)}) async-start(bf16[3,2240,1120]{2,0,1:T(4,128)(2,1)} %bitcast.65), calls=%async_computation | async-start | bytes 41287680 | tf_op jit(solution)/shard_map/all_to_all | solution.py:14
  54.5 1.9 fusion.7
  56.4 261.0 %all-to-all-done = bf16[3,2240,1120]{2,0,1:T(4,128)(2,1)} async-done(((bf16[3,2240,1120]{2,0,1:T(4,128)(2,1)}), bf16[3,2240,1120]{2,0,1:T(4,128)(2,1)}, u32[]{:S(2)}, u32[]{:S(2)}) %all-to-all-start) | async-done | bytes 15052832 | tf_op jit(solution)/shard_map/all_to_all | solution.py:14
  317.3 14.1 %fusion.3 = f32[3,448,1120]{2,1,0:T(8,128)S(1)} fusion(bf16[3,2240,1120]{2,0,1:T(4,128)(2,1)} %all-to-all-done, bf16[448,2240]{1,0:T(8,128)(2,1)} %fusion.7), kind=kOutput, calls=%fused_computation.5 | convolution fusion | flops 6743654400 | bytes 23080960 | tf_op jit(solution)/shard_map/rn,cnh->crh/dot_general | solution.py:83
  331.4 1.4 fusion.13
  332.8 1.5 copy-done.2
  334.3 3.4 reshape.88
  337.8 3.1 reshape.87
  340.9 3.1 fusion.16
  344.7 70.7 %all-reduce.6.cloned.1.call-done = f32[2,10,112,112]{3,2,1,0:T(8,128)} async-done(((f32[2,10,112,112]{3,2,1,0:T(8,128)}), f32[2,10,112,112]{3,2,1,0:T(8,128)}) %all-reduce.6.cloned.1.call-update) | async-done | bytes 1003536 | tf_op jit(solution)/shard_map/psum | solution.py:95
  415.4 4.8 fusion.20
  425.0 1.3 fusion.27
  426.3 1.3 dynamic-update-slice.2
  427.6 63.4 %all-reduce.3 = (bf16[32]{0:T(256)(128)(2,1)S(1)}, bf16[32]{0:T(256)(128)(2,1)S(1)}, bf16[32]{0:T(256)(128)(2,1)S(1)}) all-reduce(bf16[32]{0:T(256)(128)(2,1)S(1)} %dynamic-update-slice, bf16[32]{0:T(256)(128)(2,1)S(1)} %dynamic-update-slice.1, bf16[32]{0:T(256)(128)(2,1)S(1)} %dynamic-update-slice.2), channel_id=1, replica_groups=mesh['tm'=32,'space'=8] {'tm'}, use_global_device_ids=true, to_apply=%add | all-reduce | flops 96 | bytes 384
  492.4 1.8 slice_maximum_fusion
  494.1 3.3 reshape.89
  497.5 193.3 %while.32 = (s32[]{:T(128)}, f32[]{:T(128)}, f32[]{:T(128)}, f32[10,112,112]{2,1,0:T(8,128)S(1)}, s32[]{:T(128)}, /*index=5*/bf16[32]{0:T(256)(128)(2,1)S(1)}, b...) while((s32[]{:T(128)}, f32[]{:T(128)}, f32[]{:T(128)}, ...), condition=%wide.region_7.8_spmd, body=%wide.region_6.7_spmd.sunk | while | flops 501773 | bytes 1254722 | solution.py:51
  502.4 1.3 fusion.33
  508.7 1.3 fusion.33
  514.9 1.3 fusion.33
  521.1 1.3 fusion.33
  527.4 1.3 fusion.33
  533.7 1.3 fusion.33
  539.9 1.3 fusion.33
  546.1 1.3 fusion.33
  552.3 1.3 fusion.33
  558.6 1.3 fusion.33
  564.9 1.3 fusion.33
  571.2 1.3 fusion.33
  577.4 1.3 fusion.33
  583.6 1.3 fusion.33
  589.8 1.3 fusion.33
  596.1 1.3 fusion.33
  602.3 1.3 fusion.33
  608.5 1.3 fusion.33
  614.7 1.3 fusion.33
  621.0 1.3 fusion.33
  627.2 1.3 fusion.33
  633.4 1.3 fusion.33
  639.6 1.3 fusion.33
  645.9 1.3 fusion.33
  652.1 1.3 fusion.33
  658.3 1.3 fusion.33
  664.6 1.3 fusion.33
  670.8 1.3 fusion.33
  677.0 1.3 fusion.33
  683.2 1.3 fusion.33
  689.5 1.3 fusion.33
  690.8 38.9 %while.33 = (s32[]{:T(128)}, f32[10,112,112]{2,1,0:T(8,128)S(1)}, s32[]{:T(128)}, f32[32,10,112,112]{3,2,1,0:T(8,128)}, s32[]{:T(128)}, /*index=5*/s32[]{:T(128)}) while((s32[]{:T(128)}, f32[10,112,112]{2,1,0:T(8,128)S(1)}, s32[]{:T(128)}, f32[32,10,112,112]{3,2,1,0:T(8,128)}, s32[]{:T(128)}, /*index=5*/s32[]{:T(128)}) %tuple.71), condition=%wide.region_4.5_spmd.clone, body=%wide.region_3.4_spmd.clone.sunk | while | flops 376324 | bytes 1505381 | solution.py:26
  690.8 1.3 add_select_fusion.2
  692.2 1.2 add_select_fusion.2
  693.4 1.2 add_select_fusion.2
  694.7 1.2 add_select_fusion.2
  695.9 1.2 add_select_fusion.2
  697.2 1.2 add_select_fusion.2
  698.4 1.2 add_select_fusion.2
  699.7 1.2 add_select_fusion.2
  712.2 1.2 add_select_fusion.2
  729.8 3.3 fusion.15
  733.1 5.1 fusion.8
  738.5 1.4 copy.50
  (161 shorter events, 90.5 us)
Async XLA Ops:
  46.2 7.6 %copy-start.1 = (bf16[2,224,2240]{2,1,0:T(8,128)(2,1)S(1)}, bf16[2,224,2240]{2,1,0:T(8,128)(2,1)}, u32[]{:S(2)}) copy-start(bf16[2,224,2240]{2,1,0:T(8,128)(2,1)} %param.11) | copy-start | bytes 6021124
  46.2 271.1 %all-to-all-start = ((bf16[3,2240,1120]{2,0,1:T(4,128)(2,1)}), bf16[3,2240,1120]{2,0,1:T(4,128)(2,1)}, u32[]{:S(2)}, u32[]{:S(2)}) async-start(bf16[3,2240,1120]{2,0,1:T(4,128)(2,1)} %bitcast.65), calls=%async_computation | async-start | bytes 41287680 | tf_op jit(solution)/shard_map/all_to_all | solution.py:14
  53.8 0.7 copy-start.5
  53.8 361.6 %all-reduce.6.cloned.1.call-start = ((), (), s32[]{:S(2)}) async-start(), calls=%async_computation.1 | async-start | bytes 2293760 | tf_op jit(solution)/shard_map/psum | solution.py:95
  331.4 2.9 copy-start.2
  340.9 3.2 copy-start.7
  344.0 153.4 %all-gather.7.cloned.1.call-start = ((), (), s32[]{:S(2)}) async-start(), calls=%async_computation.3 | async-start | bytes 9461760 | tf_op jit(solution)/shard_map/all_gather | solution.py:34
  415.4 5.8 copy-start.3
  420.2 2.7 copy-start.8
  420.2 71.5 %copy-start.6 = (f32[1120]{0:T(1024)S(1)}, f32[1120]{0:T(1024)}, u32[]{:S(2)}) copy-start(f32[1120]{0:T(1024)} %param.16) | copy-start | bytes 13444
  421.0 269.8 %all-gather.5.cloned.1.call-start = ((), (), s32[]{:S(2)}) async-start(), calls=%async_computation.2 | async-start | bytes 18923520 | tf_op jit(solution)/shard_map/all_gather | solution.py:19
  690.8 38.9 %copy-start.4 = (f32[2,10,112,112]{3,2,1,0:T(8,128)S(1)}, f32[2,10,112,112]{3,2,1,0:T(8,128)}, u32[]{:S(2)}) copy-start(f32[2,10,112,112]{3,2,1,0:T(8,128)} %all-reduce.6.cloned.1.call-done) | copy-start | bytes 3010564
  729.8 3.3 copy-start
Sparse Core Ops, SparseCore 0:
  344.1 71.1 all-reduce.5
  421.1 58.7 all-gather.6
  482.5 80.7 all-gather.4
